TPU v7x, 32 devices: a whole 2x2x4 slice. The times are simulated.
32 devices in a mesh: row: 8 (over z, x), col: 4 (over y, core).
Axes of the slice: x: 2, y: 2, z: 4, core: 2. Of those that a mesh axis runs over, the one named last changes fastest.
Arguments:
- tokens: bfloat16 [512, 4096], P('row', 'col'), may hold values from -6 to 6
- gate_weight: bfloat16 [4096, 14336], P('col', 'row'), may hold values from -0.09375 to 0.09375
- up_weight: bfloat16 [4096, 14336], P('col', 'row'), may hold values from -0.09375 to 0.09375
- down_weight: bfloat16 [14336, 4096], P('row', 'col'), may hold values from -0.046875 to 0.046875
- gate_mask: int32 [32, 112], replicated, may hold values 0 or 1
- up_mask: int32 [32, 112], replicated, may hold values 0 or 1
- down_mask: int32 [112, 32], replicated, may hold values 0 or 1
- out_grad: bfloat16 [512, 4096], P('row', 'col'), may hold values from -6 to 6
Outputs:
- mixed: bfloat16 [512, 4096], P('row', 'col')
- input_grad: bfloat16 [512, 4096], P('row', 'col')
- gate_grad: float32 [4096, 14336], P('col', 'row')
- up_grad: float32 [4096, 14336], P('col', 'row')
- down_grad: float32 [14336, 4096], P('row', 'col')
All inputs are finite; a program needn't handle non-finite values.
Results may differ from a plain program's by a relative error of at most 0.0049.
Values may be sent and summed in bfloat16 or wider, within the bound.
No kernel may reach another device: no remote copies, remote signals or barrier semaphores. Data moves between devices by JAX's collectives and lax.ppermute only.
A program may use at most 128 MiB of HBM per device.

v0:
```python
import jax
import jax.numpy as jnp
from jax import lax
from jax.sharding import PartitionSpec as P

BLOCK = 128


def expand_mask(mask, row_start, row_count, col_start, col_count):
    row_block = (row_start + lax.broadcasted_iota(jnp.int32, (row_count, 1), 0)) // BLOCK
    left = (row_block == lax.broadcasted_iota(jnp.int32, (1, mask.shape[0]), 1)).astype(jnp.float32)
    col_block = (col_start + lax.broadcasted_iota(jnp.int32, (1, col_count), 1)) // BLOCK
    right = (lax.broadcasted_iota(jnp.int32, (mask.shape[1], 1), 0) == col_block).astype(
        jnp.float32
    )
    middle = jnp.dot(left, mask.astype(jnp.float32), precision=lax.Precision.HIGHEST)
    return jnp.dot(middle, right, precision=lax.Precision.HIGHEST)


def contract_first(left, right):
    return lax.dot_general(
        left, right, (((0,), (0,)), ((), ())), preferred_element_type=jnp.float32
    )


def contract_last(left, right):
    return lax.dot_general(
        left, right, (((1,), (1,)), ((), ())), preferred_element_type=jnp.float32
    )


def per_device(
    tokens, gate_weight, up_weight, down_weight, gate_mask, up_mask, down_mask, out_grad
):
    row_index = lax.axis_index("row")
    col_index = lax.axis_index("col")
    feat_cols = gate_weight.shape[0]
    unit_cols = gate_weight.shape[1]
    keep_gate = expand_mask(
        gate_mask, col_index * feat_cols, feat_cols, row_index * unit_cols, unit_cols
    )
    keep_up = expand_mask(
        up_mask, col_index * feat_cols, feat_cols, row_index * unit_cols, unit_cols
    )
    keep_down = expand_mask(
        down_mask, row_index * unit_cols, unit_cols, col_index * feat_cols, feat_cols
    )
    zero = jnp.zeros((), jnp.bfloat16)
    kept_both = jnp.concatenate(
        [jnp.where(keep_gate > 0, gate_weight, zero), jnp.where(keep_up > 0, up_weight, zero)],
        axis=1,
    )
    kept_down = jnp.where(keep_down > 0, down_weight, zero)
    gathered = lax.all_gather(tokens, "row", axis=0, tiled=True)
    block = gathered
    both = lax.psum_scatter(
        jnp.dot(block, kept_both, preferred_element_type=jnp.float32),
        "col",
        scatter_dimension=0,
        tiled=True,
    )
    gate = both[:, :unit_cols]
    up_part = both[:, unit_cols:]
    sig = jax.nn.sigmoid(gate)
    hidden = (gate * sig * up_part).astype(jnp.bfloat16)
    hidden_all = lax.all_gather(hidden, "col", axis=0, tiled=True)
    block = hidden_all
    mixed = lax.psum_scatter(
        jnp.dot(block, kept_down, preferred_element_type=jnp.float32),
        "row",
        scatter_dimension=0,
        tiled=True,
    ).astype(jnp.bfloat16)
    grad_all = lax.all_gather(out_grad, "row", axis=0, tiled=True)
    down_grad = keep_down * contract_first(hidden_all, grad_all)
    block = grad_all
    hidden_grad = lax.psum_scatter(
        contract_last(block, kept_down), "col", scatter_dimension=0, tiled=True
    )
    dgate = hidden_grad * up_part * sig * (1.0 + gate * (1.0 - sig))
    dup = hidden_grad * gate * sig
    pre_grad = jnp.concatenate([dgate.astype(jnp.bfloat16), dup.astype(jnp.bfloat16)], axis=1)
    pre_all = lax.all_gather(pre_grad, "col", axis=0, tiled=True)
    weight_both = contract_first(gathered, pre_all)
    gate_grad = keep_gate * weight_both[:, :unit_cols]
    up_grad = keep_up * weight_both[:, unit_cols:]
    block = pre_all
    input_grad = lax.psum_scatter(
        contract_last(block, kept_both), "row", scatter_dimension=0, tiled=True
    ).astype(jnp.bfloat16)
    return (mixed, input_grad, gate_grad, up_grad, down_grad)


def solution(mesh):
    return jax.shard_map(
        per_device,
        mesh=mesh,
        in_specs=(
            P("row", "col"),
            P("col", "row"),
            P("col", "row"),
            P("row", "col"),
            P(),
            P(),
            P(),
            P("row", "col"),
        ),
        out_specs=(
            P("row", "col"),
            P("row", "col"),
            P("col", "row"),
            P("col", "row"),
            P("row", "col"),
        ),
        check_vma=False,
    )
```

profile of v0, /device:TPU:0, one launch (start us, length us, event | category | flops | bytes accessed | tf_op | source)
XLA Modules:
  0.0 412.9 jit_solution(11120879040870394195)
XLA Ops:
  7.9 0.7 all-gather.5.cloned.1.call-update
  8.7 1.4 fusion.1
  10.1 5.0 %fusion.11 = f32[1792,1024]{1,0:T(8,128)} fusion(f32[1792,32]{1,0:T(8,128)S(1)} %fusion.1, s32[1024]{0:T(1024)S(1)} %add_select_fusion.1), kind=kOutput, calls=%fused_computation.30 | convolution fusion | flops 704675840 | bytes 7573504 | tf_op jit(solution)/shard_map/dot_general | solution.py:17
  15.2 38.0 %all-gather.9.cloned.1.call-done = bf16[512,1024]{1,0:T(8,128)(2,1)} async-done(((bf16[64,1024]{1,0:T(8,128)(2,1)}), bf16[512,1024]{1,0:T(8,128)(2,1)}) %all-gather.9.cloned.1.call-update) | async-done | bytes 1048592 | tf_op jit(solution)/shard_map/all_gather | solution.py:74
  53.1 8.3 %convolution_bitcast_fusion.2 = f32[512,1792]{0,1:T(8,128)} fusion(bf16[512,1024]{1,0:T(8,128)(2,1)} %all-gather.9.cloned.1.call-done, bf16[1792,1024]{1,0:T(8,128)(2,1)} %param.11, f32[1792,1024]{1,0:T(8,128)} %fusion.11), kind=kOutput, calls=%fused_computation.10 | convolution fusion | flops 1882718208 | bytes 15728640 | tf_op jit(solution)/shard_map/dot_general | solution.py:27
  63.1 7.6 %compare_select_fusion.2 = (bf16[1024,1792]{1,0:T(8,128)(2,1)}, f32[1024,1792]{1,0:T(8,128)}) fusion(bf16[1024,1792]{1,0:T(8,128)(2,1)} %param.9, f32[1024,112]{1,0:T(8,128)S(1)} %fusion.5, s32[1792]{0:T(1024)S(1)} %add_select_fusion), kind=kOutput, calls=%fused_computation.6 | convolution fusion | flops 2470121472 | bytes 15145984 | tf_op jit(solution)/shard_map/dot_general | solution.py:17
  70.7 5.9 %compare_select_fusion.1 = (bf16[1024,1792]{1,0:T(8,128)(2,1)}, f32[1024,1792]{1,0:T(8,128)}) fusion(bf16[1024,1792]{1,0:T(8,128)(2,1)S(1)} %copy-done, f32[1024,112]{1,0:T(8,128)S(1)} %fusion.4, s32[1792]{0:T(1024)S(1)} %add_select_fusion), kind=kOutput, calls=%fused_computation.5 | convolution fusion | flops 2470121472 | bytes 15145984 | tf_op jit(solution)/shard_map/dot_general | solution.py:17
  76.6 17.7 %all-gather.5.cloned.1.call-done = bf16[512,1024]{1,0:T(8,128)(2,1)} async-done(((bf16[64,1024]{1,0:T(8,128)(2,1)}), bf16[512,1024]{1,0:T(8,128)(2,1)}) %all-gather.5.cloned.1.call-update) | async-done | bytes 1048592 | tf_op jit(solution)/shard_map/all_gather | solution.py:54
  94.3 11.0 %convolution_bitcast_fusion.1 = f32[512,3584]{0,1:T(8,128)} fusion(bf16[512,1024]{1,0:T(8,128)(2,1)} %all-gather.5.cloned.1.call-done, bf16[1024,1792]{1,0:T(8,128)(2,1)} %get-tuple-element.10, bf16[1024,1792]{1,0:T(8,128)(2,1)} %get-tuple-element.12), kind=kOutput, calls=%fused_computation.7 | convolution fusion | flops 3772776448 | bytes 15728640 | tf_op jit(solution)/shard_map/dot_general | solution.py:57
  105.3 31.3 %reduce-scatter.9.cloned.1.call-done = f32[128,1792]{0,1:T(8,128)} async-done(((f32[512,1792]{0,1:T(8,128)}), f32[128,1792]{0,1:T(8,128)}) %reduce-scatter.9.cloned.1.call-update) | async-done | bytes 917520 | tf_op jit(solution)/shard_map/reduce_scatter | solution.py:77
  136.6 67.0 %reduce-scatter.5.cloned.1.call-done = f32[128,3584]{0,1:T(8,128)} async-done(((f32[512,3584]{0,1:T(8,128)}), f32[128,3584]{0,1:T(8,128)}) %reduce-scatter.5.cloned.1.call-update) | async-done | bytes 1835024 | tf_op jit(solution)/shard_map/reduce_scatter | solution.py:56
  203.7 3.1 multiply_convert_fusion.1
  206.8 1.0 pad_maximum_fusion.3
  207.9 20.3 %all-gather.7.cloned.1.call-done = bf16[512,1792]{0,1:T(8,128)(2,1)} async-done(((bf16[128,1792]{0,1:T(8,128)(2,1)}), bf16[512,1792]{0,1:T(8,128)(2,1)}) %all-gather.7.cloned.1.call-update) | async-done | bytes 1835024 | tf_op jit(solution)/shard_map/all_gather | solution.py:66
  228.2 8.2 %fusion.24 = f32[512,1024]{1,0:T(8,128)} fusion(bf16[512,1792]{0,1:T(8,128)(2,1)} %all-gather.7.cloned.1.call-done, bf16[1792,1024]{1,0:T(8,128)(2,1)} %param.11, f32[1792,1024]{1,0:T(8,128)} %fusion.11), kind=kOutput, calls=%fused_computation.55 | convolution fusion | flops 1882718208 | bytes 14942208 | tf_op jit(solution)/shard_map/dot_general | solution.py:69
  236.7 24.9 %all-gather.11.cloned.1.call-done = bf16[512,3584]{0,1:T(8,128)(2,1)} async-done(((bf16[128,3584]{0,1:T(8,128)(2,1)}), bf16[512,3584]{0,1:T(8,128)(2,1)}) %all-gather.11.cloned.1.call-update) | async-done | bytes 3670032 | tf_op jit(solution)/shard_map/all_gather | solution.py:83
  261.6 9.5 %fusion = f32[512,1024]{1,0:T(8,128)} fusion(bf16[512,3584]{0,1:T(8,128)(2,1)} %all-gather.11.cloned.1.call-done, bf16[1024,1792]{1,0:T(8,128)(2,1)} %get-tuple-element.10, bf16[1024,1792]{1,0:T(8,128)(2,1)} %get-tuple-element.12), kind=kOutput, calls=%fused_computation.8 | convolution fusion | flops 3772776448 | bytes 13107200 | tf_op jit(solution)/shard_map/dot_general | solution.py:27
  271.2 9.4 %convolution_multiply_fusion = f32[1792,1024]{1,0:T(8,128)} fusion(f32[1792,1024]{1,0:T(8,128)} %fusion.11, bf16[512,1792]{0,1:T(8,128)(2,1)} %all-gather.7.cloned.1.call-done, bf16[512,1024]{1,0:T(8,128)(2,1)} %all-gather.9.cloned.1.call-done), kind=kOutput, calls=%fused_computation.9 | convolution fusion | flops 1880883200 | bytes 17563648 | tf_op jit(solution)/shard_map/dot_general | solution.py:21
  280.6 7.6 %convolution_bitcast_fusion = f32[1024,3584]{1,0:T(8,128)} fusion(bf16[512,3584]{0,1:T(8,128)(2,1)S(1)} %copy-done.3, bf16[512,1024]{1,0:T(8,128)(2,1)S(1)} %copy-done.4), kind=kOutput, calls=%fused_computation | convolution fusion | flops 3758096384 | bytes 19398656 | tf_op jit(solution)/shard_map/dot_general | solution.py:21
  288.2 14.1 %slice_multiply_fusion = (f32[1024,1792]{1,0:T(8,128)}, f32[1024,1792]{1,0:T(8,128)}) fusion(f32[1024,1792]{1,0:T(8,128)} %get-tuple-element.11, f32[1024,3584]{1,0:T(8,128)} %convolution_bitcast_fusion, f32[1024,1792]{1,0:T(8,128)S(1)} %bitcast.18), kind=kLoop, calls=%fused_computation.1 | loop fusion | flops 3670016 | bytes 44040192 | tf_op jit(solution)/shard_map/mul | solution.py:86
  302.3 31.2 %reduce-scatter.7.cloned.1.call-done = f32[64,1024]{1,0:T(8,128)} async-done(((f32[512,1024]{1,0:T(8,128)}), f32[64,1024]{1,0:T(8,128)}) %reduce-scatter.7.cloned.1.call-update) | async-done | bytes 262160 | tf_op jit(solution)/shard_map/reduce_scatter | solution.py:68
  333.5 1.6 convert_element_type.34
  335.1 69.3 %reduce-scatter.11.cloned.1.call-done = f32[64,1024]{1,0:T(8,128)} async-done(((f32[512,1024]{1,0:T(8,128)}), f32[64,1024]{1,0:T(8,128)}) %reduce-scatter.11.cloned.1.call-update) | async-done | bytes 262160 | tf_op jit(solution)/shard_map/reduce_scatter | solution.py:88
  404.5 1.6 convert_element_type.37
  (34 shorter events, 2.9 us)
Async XLA Ops:
  7.2 46.0 %all-gather.9.cloned.1.call-start = ((), (), s32[]{:S(2)}) async-start(), calls=%async_computation.8 | async-start | bytes 1179648 | tf_op jit(solution)/shard_map/all_gather | solution.py:74
  7.9 86.4 %all-gather.5.cloned.1.call-start = ((), (), s32[]{:S(2)}) async-start(), calls=%async_computation.4 | async-start | bytes 1179648 | tf_op jit(solution)/shard_map/all_gather | solution.py:54
  8.7 128.0 %reduce-scatter.9.cloned.1.call-start = ((), (), s32[]{:S(2)}) async-start(), calls=%async_computation.9 | async-start | bytes 4587520 | tf_op jit(solution)/shard_map/reduce_scatter | solution.py:77
  61.4 0.7 copy-start.1
  61.4 1.2 copy-start.2
  61.4 142.2 %reduce-scatter.5.cloned.1.call-start = ((), (), s32[]{:S(2)}) async-start(), calls=%async_computation.5 | async-start | bytes 9175040 | tf_op jit(solution)/shard_map/reduce_scatter | solution.py:56
  63.1 7.6 %copy-start = (bf16[1024,1792]{1,0:T(8,128)(2,1)S(1)}, bf16[1024,1792]{1,0:T(8,128)(2,1)}, u32[]{:S(2)}) copy-start(bf16[1024,1792]{1,0:T(8,128)(2,1)} %param.10) | copy-start | bytes 11010052
  105.3 123.0 %all-gather.7.cloned.1.call-start = ((), (), s32[]{:S(2)}) async-start(), calls=%async_computation.6 | async-start | bytes 2293760 | tf_op jit(solution)/shard_map/all_gather | solution.py:66
  206.8 54.9 %all-gather.11.cloned.1.call-start = ((), (), s32[]{:S(2)}) async-start(), calls=%async_computation.10 | async-start | bytes 4587520 | tf_op jit(solution)/shard_map/all_gather | solution.py:83
  207.9 125.6 %reduce-scatter.7.cloned.1.call-start = ((), (), s32[]{:S(2)}) async-start(), calls=%async_computation.7 | async-start | bytes 2359296 | tf_op jit(solution)/shard_map/reduce_scatter | solution.py:68
  236.4 168.0 %reduce-scatter.11.cloned.1.call-start = ((), (), s32[]{:S(2)}) async-start(), calls=%async_computation.11 | async-start | bytes 2359296 | tf_op jit(solution)/shard_map/reduce_scatter | solution.py:88
  271.2 17.0 %slice-start = ((s8[7340032]{0:T(1024)(128)(4,1)}), s8[3145728]{0:T(1024)(128)(4,1)S(1)}, s32[]{:S(2)}) async-start(s8[7340032]{0:T(1024)(128)(4,1)} %bitcast.17), calls=%async_computation.12 | async-start | bytes 6291456
  271.2 9.4 %copy-start.3 = (bf16[512,3584]{0,1:T(8,128)(2,1)S(1)}, bf16[512,3584]{0,1:T(8,128)(2,1)}, u32[]{:S(2)}) copy-start(bf16[512,3584]{0,1:T(8,128)(2,1)} %all-gather.11.cloned.1.call-done) | copy-start | bytes 11010052
  271.2 9.4 %copy-start.4 = (bf16[512,1024]{1,0:T(8,128)(2,1)S(1)}, bf16[512,1024]{1,0:T(8,128)(2,1)}, u32[]{:S(2)}) copy-start(bf16[512,1024]{1,0:T(8,128)(2,1)} %all-gather.5.cloned.1.call-done) | copy-start | bytes 3145732
  271.2 17.0 %slice-start.1 = ((s8[7340032]{0:T(1024)(128)(4,1)}), s8[4194304]{0:T(1024)(128)(4,1)S(1)}, s32[]{:S(2)}) async-start(s8[7340032]{0:T(1024)(128)(4,1)} %bitcast.17), calls=%async_computation.13 | async-start | bytes 8388608
Sparse Core Ops, SparseCore 0:
  10.1 42.9 all-gather.8
  55.3 38.9 all-gather.4
  96.8 39.7 reduce-scatter.8
  139.0 64.6 reduce-scatter.4
  206.9 21.3 all-gather.6
  229.6 31.9 all-gather.10
  265.2 68.2 reduce-scatter.6
  337.0 67.3 reduce-scatter.10
where the time goes:
time: 413 us
  waiting for transfers between devices  301 us (73%)
  matrix products  74.7 us (18%)
  other arithmetic  21.4 us (5%)
  between operations  14.2 us (3%)
    reduce_scatter x1, waiting for transfers between devices, per_device(): lax.psum_scatter(contract_last(block, kept_both), 'row', scatter_dimensio...  69.3 us
    reduce_scatter x1, waiting for transfers between devices, per_device(): lax.psum_scatter(jnp.dot(block, kept_both, preferred_element_type=jnp.flo...  67 us
    all_gather x1, waiting for transfers between devices, per_device(): grad_all = lax.all_gather(out_grad, 'row', axis=0, tiled=True)  38 us
    reduce_scatter x1, waiting for transfers between devices, per_device(): lax.psum_scatter(contract_last(block, kept_down), 'col', scatter_dimensio...  31.3 us
    reduce_scatter x1, waiting for transfers between devices, per_device(): lax.psum_scatter(jnp.dot(block, kept_down, preferred_element_type=jnp.flo...  31.2 us
    all_gather x1, waiting for transfers between devices, per_device(): pre_all = lax.all_gather(pre_grad, 'col', axis=0, tiled=True)  24.9 us
    all_gather x1, waiting for transfers between devices, per_device(): hidden_all = lax.all_gather(hidden, 'col', axis=0, tiled=True)  20.3 us
    dot_general x3, matrix products, expand_mask(): return jnp.dot(middle, right, precision=lax.Precision.HIGHEST)  18.6 us
  transfers between devices with their start and end apart: 8, of which 8 were waited for; matrix products, arithmetic and copies ran while one was open for 22% of the time, Pallas kernels for 0%

commit v1 on v0

--- a/solution.py
+++ b/solution.py
@@ -4,6 +4,18 @@
 from jax.sharding import PartitionSpec as P
 
 BLOCK = 128
+
+
+def doubled_up(array, axis, dim):
+    ways, here, step = (lax.axis_size(axis), lax.axis_index(axis), array.shape[dim])
+    line, have = (array, 1)
+    while have < ways:
+        line = jnp.concatenate(
+            [line, lax.ppermute(line, axis, [(d, (d - have) % ways) for d in range(ways)])],
+            axis=dim,
+        )
+        have = 2 * have
+    return jnp.roll(line, here * step, axis=dim)
 
 
 def expand_mask(mask, row_start, row_count, col_start, col_count):
@@ -80,7 +92,7 @@
     dgate = hidden_grad * up_part * sig * (1.0 + gate * (1.0 - sig))
     dup = hidden_grad * gate * sig
     pre_grad = jnp.concatenate([dgate.astype(jnp.bfloat16), dup.astype(jnp.bfloat16)], axis=1)
-    pre_all = lax.all_gather(pre_grad, "col", axis=0, tiled=True)
+    pre_all = doubled_up(pre_grad, "col", 0)
     weight_both = contract_first(gathered, pre_all)
     gate_grad = keep_gate * weight_both[:, :unit_cols]
     up_grad = keep_up * weight_both[:, unit_cols:]

time: 413 us -> 389 us (0.942)
  waiting for transfers between devices: 301 us -> 269 us
  local copies, waits for them, and re-layouts: 0.49 us -> 5.49 us
  other arithmetic: 21.4 us -> 26.1 us
    ppermute x0 -> x2, waiting for transfers between devices: none -> 49.6 us  [doubled_up(): lax.ppermute(line, axis, [(d, (d - have) % ways) for d in range(ways)])]
    reduce_scatter x1, waiting for transfers between devices: 31.2 us -> 0.01 us  [per_device(): lax.psum_scatter(jnp.dot(block, kept_down, preferred_element_type=jnp.flo...]
    all_gather x1 -> x0, waiting for transfers between devices: 24.9 us -> none  [per_device(): pre_all = lax.all_gather(pre_grad, 'col', axis=0, tiled=True)]
    all_gather x1, waiting for transfers between devices: 20.3 us -> 2.79 us  [per_device(): hidden_all = lax.all_gather(hidden, 'col', axis=0, tiled=True)]
    reduce_scatter x1, waiting for transfers between devices: 69.3 us -> 60.9 us  [per_device(): lax.psum_scatter(contract_last(block, kept_both), 'row', scatter_dimensio...]
  transfers between devices with their start and end apart: 8 -> 9, of which waited for: 8 -> 8; matrix products, arithmetic and copies ran while one was open for 22% -> 25% of each run, Pallas kernels for 0% -> 0%
where the time goes in v1:
time: 389 us; the launch traced here: 388 us
  waiting for transfers between devices  269 us (69%)
  matrix products  72.6 us (19%)
  other arithmetic  26.1 us (7%)
  between operations  14.3 us (4%)
  local copies, waits for them, and re-layouts  5.49 us (1%)
    reduce_scatter x1, waiting for transfers between devices, per_device(): lax.psum_scatter(jnp.dot(block, kept_both, preferred_element_type=jnp.flo...  67 us
    reduce_scatter x1, waiting for transfers between devices, per_device(): lax.psum_scatter(contract_last(block, kept_both), 'row', scatter_dimensio...  60.9 us
    ppermute x2, waiting for transfers between devices, doubled_up(): lax.ppermute(line, axis, [(d, (d - have) % ways) for d in range(ways)])  49.6 us
    all_gather x1, waiting for transfers between devices, per_device(): grad_all = lax.all_gather(out_grad, 'row', axis=0, tiled=True)  38 us
    reduce_scatter x1, waiting for transfers between devices, per_device(): lax.psum_scatter(contract_last(block, kept_down), 'col', scatter_dimensio...  31.3 us
    dot_general x3, matrix products, expand_mask(): return jnp.dot(middle, right, precision=lax.Precision.HIGHEST)  18.6 us
    all_gather x1, waiting for transfers between devices, per_device(): gathered = lax.all_gather(tokens, 'row', axis=0, tiled=True)  17.7 us
    dot_general x2, matrix products, contract_first(): lax.dot_general(left, right, (((0,), (0,)), ((), ())), preferred_element_...  16.8 us
  transfers between devices with their start and end apart: 9, of which 8 were waited for; matrix products, arithmetic and copies ran while one was open for 25% of the time, Pallas kernels for 0%

profile of v1, /device:TPU:0, one launch (start us, length us, event | category | flops | bytes accessed | tf_op | source)
XLA Modules:
  0.0 388.4 jit_solution(2181843242203250253)
XLA Ops:
  10.1 5.0 %fusion.13 = f32[1792,1024]{1,0:T(8,128)} fusion(f32[1792,32]{1,0:T(8,128)S(1)} %fusion.3, s32[1024]{0:T(1024)S(1)} %add_select_fusion.1), kind=kOutput, calls=%fused_computation.33 | convolution fusion | flops 704675840 | bytes 7573504 | tf_op jit(solution)/shard_map/dot_general | solution.py:29
  15.2 38.0 %all-gather.8.cloned.1.call-done = bf16[512,1024]{1,0:T(8,128)(2,1)} async-done(((bf16[64,1024]{1,0:T(8,128)(2,1)}), bf16[512,1024]{1,0:T(8,128)(2,1)}) %all-gather.8.cloned.1.call-update) | async-done | bytes 1048592 | tf_op jit(solution)/shard_map/all_gather | solution.py:86
  53.1 8.3 %convolution_bitcast_fusion.2 = f32[512,1792]{0,1:T(8,128)} fusion(bf16[512,1024]{1,0:T(8,128)(2,1)} %all-gather.8.cloned.1.call-done, bf16[1792,1024]{1,0:T(8,128)(2,1)} %param.11, f32[1792,1024]{1,0:T(8,128)} %fusion.13), kind=kOutput, calls=%fused_computation.10 | convolution fusion | flops 1882718208 | bytes 15728640 | tf_op jit(solution)/shard_map/dot_general | solution.py:39
  63.1 7.6 %compare_select_fusion.2 = (bf16[1024,1792]{1,0:T(8,128)(2,1)}, f32[1024,1792]{1,0:T(8,128)}) fusion(bf16[1024,1792]{1,0:T(8,128)(2,1)} %param.9, f32[1024,112]{1,0:T(8,128)S(1)} %fusion.7, s32[1792]{0:T(1024)S(1)} %add_select_fusion), kind=kOutput, calls=%fused_computation.6 | convolution fusion | flops 2470121472 | bytes 15145984 | tf_op jit(solution)/shard_map/dot_general | solution.py:29
  70.7 5.9 %compare_select_fusion.1 = (bf16[1024,1792]{1,0:T(8,128)(2,1)}, f32[1024,1792]{1,0:T(8,128)}) fusion(bf16[1024,1792]{1,0:T(8,128)(2,1)S(1)} %copy-done.4, f32[1024,112]{1,0:T(8,128)S(1)} %fusion.6, s32[1792]{0:T(1024)S(1)} %add_select_fusion), kind=kOutput, calls=%fused_computation.5 | convolution fusion | flops 2470121472 | bytes 15145984 | tf_op jit(solution)/shard_map/dot_general | solution.py:29
  76.6 17.7 %all-gather.4.cloned.1.call-done = bf16[512,1024]{1,0:T(8,128)(2,1)} async-done(((bf16[64,1024]{1,0:T(8,128)(2,1)}), bf16[512,1024]{1,0:T(8,128)(2,1)}) %all-gather.4.cloned.1.call-update) | async-done | bytes 1048592 | tf_op jit(solution)/shard_map/all_gather | solution.py:66
  94.3 11.0 %convolution_bitcast_fusion.1 = f32[512,3584]{0,1:T(8,128)} fusion(bf16[512,1024]{1,0:T(8,128)(2,1)} %all-gather.4.cloned.1.call-done, bf16[1024,1792]{1,0:T(8,128)(2,1)} %get-tuple-element.12, bf16[1024,1792]{1,0:T(8,128)(2,1)} %get-tuple-element.14), kind=kOutput, calls=%fused_computation.7 | convolution fusion | flops 3772776448 | bytes 15728640 | tf_op jit(solution)/shard_map/dot_general | solution.py:69
  105.3 31.3 %reduce-scatter.9.cloned.1.call-done = f32[128,1792]{0,1:T(8,128)} async-done(((f32[512,1792]{0,1:T(8,128)}), f32[128,1792]{0,1:T(8,128)}) %reduce-scatter.9.cloned.1.call-update) | async-done | bytes 917520 | tf_op jit(solution)/shard_map/reduce_scatter | solution.py:89
  136.6 67.0 %reduce-scatter.5.cloned.1.call-done = f32[128,3584]{0,1:T(8,128)} async-done(((f32[512,3584]{0,1:T(8,128)}), f32[128,3584]{0,1:T(8,128)}) %reduce-scatter.5.cloned.1.call-update) | async-done | bytes 1835024 | tf_op jit(solution)/shard_map/reduce_scatter | solution.py:68
  203.7 3.0 multiply_convert_fusion.1
  207.9 19.5 %collective-permute-done = bf16[128,3584]{0,1:T(8,128)(2,1)S(1)} collective-permute-done((bf16[128,3584]{0,1:T(8,128)(2,1)S(1)}, bf16[128,3584]{0,1:T(8,128)(2,1)S(1)}, u32[]{:S(2)}, u32[]{:S(2)}) %collective-permute-start) | collective-permute-done | bytes 917536 | tf_op jit(solution)/shard_map/ppermute | solution.py:14
  227.4 1.5 pad_maximum_fusion.3
  229.4 2.8 all-gather.6.cloned.1.call-done
  232.2 8.2 %fusion.28 = f32[512,1024]{1,0:T(8,128)} fusion(bf16[512,1792]{0,1:T(8,128)(2,1)} %all-gather.6.cloned.1.call-done, bf16[1792,1024]{1,0:T(8,128)(2,1)} %param.11, f32[1792,1024]{1,0:T(8,128)} %fusion.13), kind=kOutput, calls=%fused_computation.66 | convolution fusion | flops 1882718208 | bytes 14942208 | tf_op jit(solution)/shard_map/dot_general | solution.py:81
  241.7 30.2 %collective-permute-done.1 = bf16[256,3584]{0,1:T(8,128)(2,1)S(1)} collective-permute-done((bf16[256,3584]{0,1:T(8,128)(2,1)}, bf16[256,3584]{0,1:T(8,128)(2,1)S(1)}, u32[]{:S(2)}, u32[]{:S(2)}) %collective-permute-start.1) | collective-permute-done | bytes 1835040 | tf_op jit(solution)/shard_map/ppermute | solution.py:14
  271.9 1.4 constant_dynamic-update-slice_fusion.3
  275.4 1.4 constant_dynamic-update-slice_fusion
  276.8 7.5 %fusion = f32[512,1024]{1,0:T(8,128)} fusion(bf16[1024,1792]{1,0:T(8,128)(2,1)S(1)} %copy-done.6, bf16[1024,1792]{1,0:T(8,128)(2,1)S(1)} %copy-done.5, bf16[1024,3584]{0,1:T(8,128)(2,1)} %constant_dynamic-update-slice_fusion, s32[]{:T(128)S(6)} %select_n.68), kind=kOutput, calls=%fused_computation.8 | convolution fusion | flops 3772776448 | bytes 13107204 | tf_op jit(solution)/shard_map/dot_general | solution.py:39
  284.3 11.7 %convolution_bitcast_fusion = f32[1024,3584]{1,0:T(8,128)} fusion(bf16[512,1024]{1,0:T(8,128)(2,1)} %all-gather.4.cloned.1.call-done, bf16[1024,3584]{0,1:T(8,128)(2,1)} %constant_dynamic-update-slice_fusion, s32[]{:T(128)S(6)} %select_n.68), kind=kOutput, calls=%fused_computation | convolution fusion | flops 3758096384 | bytes 19398660 | tf_op jit(solution)/shard_map/dot_general | solution.py:33
  296.1 5.1 %convolution_multiply_fusion = f32[1792,1024]{1,0:T(8,128)} fusion(f32[1792,1024]{1,0:T(8,128)S(1)} %bitcast.16, bf16[512,1792]{0,1:T(8,128)(2,1)S(1)} %copy-done.2, bf16[512,1024]{1,0:T(8,128)(2,1)S(1)} %copy-done.3), kind=kOutput, calls=%fused_computation.9 | convolution fusion | flops 1880883200 | bytes 17563648 | tf_op jit(solution)/shard_map/dot_general | solution.py:33
  301.2 16.2 %slice_multiply_fusion = (f32[1024,1792]{1,0:T(8,128)}, f32[1024,1792]{1,0:T(8,128)}) fusion(f32[1024,1792]{1,0:T(8,128)} %get-tuple-element.13, f32[1024,3584]{1,0:T(8,128)} %convolution_bitcast_fusion, f32[1024,1792]{1,0:T(8,128)} %get-tuple-element.15), kind=kLoop, calls=%fused_computation.1 | loop fusion | flops 3670016 | bytes 44040192 | tf_op jit(solution)/shard_map/mul | solution.py:98
  317.4 1.6 convert_element_type.34
  319.0 60.9 %reduce-scatter.11.cloned.1.call-done = f32[64,1024]{1,0:T(8,128)} async-done(((f32[512,1024]{1,0:T(8,128)}), f32[64,1024]{1,0:T(8,128)}) %reduce-scatter.11.cloned.1.call-update) | async-done | bytes 262160 | tf_op jit(solution)/shard_map/reduce_scatter | solution.py:100
  379.9 1.6 convert_element_type.37
  (49 shorter events, 9.7 us)
Async XLA Ops:
  7.2 46.0 %all-gather.8.cloned.1.call-start = ((), (), s32[]{:S(2)}) async-start(), calls=%async_computation.8 | async-start | bytes 1179648 | tf_op jit(solution)/shard_map/all_gather | solution.py:86
  7.9 86.4 %all-gather.4.cloned.1.call-start = ((), (), s32[]{:S(2)}) async-start(), calls=%async_computation.4 | async-start | bytes 1179648 | tf_op jit(solution)/shard_map/all_gather | solution.py:66
  8.7 128.0 %reduce-scatter.9.cloned.1.call-start = ((), (), s32[]{:S(2)}) async-start(), calls=%async_computation.9 | async-start | bytes 4587520 | tf_op jit(solution)/shard_map/reduce_scatter | solution.py:89
  61.4 0.7 copy-start.7
  61.4 1.2 copy-start.8
  61.4 142.2 %reduce-scatter.5.cloned.1.call-start = ((), (), s32[]{:S(2)}) async-start(), calls=%async_computation.5 | async-start | bytes 9175040 | tf_op jit(solution)/shard_map/reduce_scatter | solution.py:68
  63.1 7.6 %copy-start.4 = (bf16[1024,1792]{1,0:T(8,128)(2,1)S(1)}, bf16[1024,1792]{1,0:T(8,128)(2,1)}, u32[]{:S(2)}) copy-start(bf16[1024,1792]{1,0:T(8,128)(2,1)} %param.10) | copy-start | bytes 11010052
  105.3 126.9 %all-gather.6.cloned.1.call-start = ((), (), s32[]{:S(2)}) async-start(), calls=%async_computation.6 | async-start | bytes 2293760 | tf_op jit(solution)/shard_map/all_gather | solution.py:78
  206.7 20.7 %copy-start = (bf16[128,1792]{0,1:T(8,128)(2,1)}, bf16[128,1792]{0,1:T(8,128)(2,1)S(1)}, u32[]{:S(2)}) copy-start(bf16[128,1792]{0,1:T(8,128)(2,1)S(1)} %get-tuple-element.8) | copy-start | bytes 1376260
  206.8 110.6 %reduce-scatter.7.cloned.1.call-start = ((), (), s32[]{:S(2)}) async-start(), calls=%async_computation.7 | async-start | bytes 2359296 | tf_op jit(solution)/shard_map/reduce_scatter | solution.py:80
  207.9 19.5 %collective-permute-start = (bf16[128,3584]{0,1:T(8,128)(2,1)S(1)}, bf16[128,3584]{0,1:T(8,128)(2,1)S(1)}, u32[]{:S(2)}, u32[]{:S(2)}) collective-permute-start(bf16[128,3584]{0,1:T(8,128)(2,1)S(1)} %get-tuple-element.10), channel_id=1, source_target_pairs={{0,3},{1,0},{2,1},{3,2},{4,7},{5,4},{6,5},{7,6},{8,11},{9,8},{10,9... | collective-permute-start | bytes 2752520 | tf_op jit(solution)/shard_map/ppermute | solution.py:14
  228.9 42.9 %collective-permute-start.1 = (bf16[256,3584]{0,1:T(8,128)(2,1)}, bf16[256,3584]{0,1:T(8,128)(2,1)S(1)}, u32[]{:S(2)}, u32[]{:S(2)}) collective-permute-start(bf16[256,3584]{0,1:T(8,128)(2,1)} %pad_maximum_fusion.3), channel_id=1, source_target_pairs={{0,2},{1,3},{2,0},{3,1},{4,6},{5,7},{6,4},{7,5},{8,10},{9,11},{10,... | collective-permute-start | bytes 5505032 | tf_op jit(solution)/shard_map/ppermute | solution.py:14
  240.4 139.6 %reduce-scatter.11.cloned.1.call-start = ((), (), s32[]{:S(2)}) async-start(), calls=%async_computation.10 | async-start | bytes 2359296 | tf_op jit(solution)/shard_map/reduce_scatter | solution.py:100
  240.6 32.7 %copy-start.1 = (bf16[128,1792]{0,1:T(8,128)(2,1)S(1)}, bf16[128,1792]{0,1:T(8,128)(2,1)}, u32[]{:S(2)}) copy-start(bf16[128,1792]{0,1:T(8,128)(2,1)} %copy-done) | copy-start | bytes 1376260
  271.9 4.9 %copy-start.6 = (bf16[1024,1792]{1,0:T(8,128)(2,1)S(1)}, bf16[1024,1792]{1,0:T(8,128)(2,1)}, u32[]{:S(2)}) copy-start(bf16[1024,1792]{1,0:T(8,128)(2,1)} %get-tuple-element.12) | copy-start | bytes 11010052
  273.3 3.5 copy-start.5
  284.3 11.8 %slice-start = ((s8[7340032]{0:T(1024)(128)(4,1)}), s8[3145728]{0:T(1024)(128)(4,1)S(1)}, s32[]{:S(2)}) async-start(s8[7340032]{0:T(1024)(128)(4,1)} %bitcast.15), calls=%async_computation.11 | async-start | bytes 6291456
  284.3 11.8 %slice-start.1 = ((s8[7340032]{0:T(1024)(128)(4,1)}), s8[4194304]{0:T(1024)(128)(4,1)S(1)}, s32[]{:S(2)}) async-start(s8[7340032]{0:T(1024)(128)(4,1)} %bitcast.15), calls=%async_computation.12 | async-start | bytes 8388608
  284.3 11.7 %copy-start.2 = (bf16[512,1792]{0,1:T(8,128)(2,1)S(1)}, bf16[512,1792]{0,1:T(8,128)(2,1)}, u32[]{:S(2)}) copy-start(bf16[512,1792]{0,1:T(8,128)(2,1)} %all-gather.6.cloned.1.call-done) | copy-start | bytes 5505028
  284.3 11.7 %copy-start.3 = (bf16[512,1024]{1,0:T(8,128)(2,1)S(1)}, bf16[512,1024]{1,0:T(8,128)(2,1)}, u32[]{:S(2)}) copy-start(bf16[512,1024]{1,0:T(8,128)(2,1)} %all-gather.8.cloned.1.call-done) | copy-start | bytes 3145732
Sparse Core Ops, SparseCore 0:
  10.1 42.9 all-gather.7
  55.3 38.9 all-gather.3
  96.8 39.7 reduce-scatter.8
  139.0 64.6 reduce-scatter.4
  206.9 25.2 all-gather.5
  240.5 68.3 reduce-scatter.6
  312.4 67.4 reduce-scatter.10
